TPU v7x, 256 devices: a whole 4x4x8 slice. The times are simulated.
256 devices in a mesh: rounds: 8 (over z), tiles: 32 (over y, x, core).
Axes of the slice: x: 4, y: 4, z: 8, core: 2. Of those that a mesh axis runs over, the one named last changes fastest.
Arguments:
- syndromes: int32 [8, 2, 8, 64, 64], P(None, None, 'rounds', 'tiles'), may hold values 0 or 1
- labels: int32 [2, 8], P(None, 'rounds'), may hold values from 0 to 1
- stab_gate: bfloat16 [64, 64, 512], P('tiles'), may hold values from -6 to 6
- bit_gate: float32 [512], replicated, may hold values from -6 to 6
- forget_bias: float32 [128], replicated, may hold values from -1 to 4
- conv_weight: bfloat16 [3, 3, 128, 512], replicated, may hold values from -0.375 to 0.375
- query: float32 [128], replicated, may hold values from -12 to 12
- readout_weight: float32 [128], replicated, may hold values from -6 to 6
Outputs:
- grad_conv: float32 [3, 3, 128, 512], replicated
- grad_stab: float32 [64, 64, 512], P('tiles')
- grad_bit: float32 [512], replicated
- grad_forget: float32 [128], replicated
- grad_query: float32 [128], replicated
- grad_readout: float32 [128], replicated
- loss: float32 [], replicated
All inputs are finite; a program needn't handle non-finite values. No bound on the sum of `syndromes` on one device may be relied on, other than what follows from the above.
Results may differ from a plain program's by a relative error of at most 0.014.
Values may be sent and summed in bfloat16 or wider, within the bound.
No kernel may reach another device: no remote copies, remote signals or barrier semaphores. Data moves between devices by JAX's collectives and lax.ppermute only.
A program may use at most 64 MiB of HBM per device.

v0:
```python
import math
import jax
import jax.numpy as jnp
from jax import lax
from jax.sharding import PartitionSpec as P


def with_halo(cells, sides, width):
    for axis, dim in sides:
        count = lax.axis_size(axis)
        ends = count - 1
        head = lax.slice_in_dim(cells, 0, width, axis=dim)
        tail = lax.slice_in_dim(cells, cells.shape[dim] - width, cells.shape[dim], axis=dim)
        cells = jnp.concatenate(
            [
                lax.ppermute(tail, axis, [(i, (i + 1) % count) for i in range(ends)]),
                cells,
                lax.ppermute(head, axis, [((i + 1) % count, i) for i in range(ends)]),
            ],
            axis=dim,
        )
    return cells


def make_patches(padded):
    row_count = padded.shape[1] - 2
    col_count = padded.shape[2] - 2
    pieces = [
        padded[:, a : a + row_count, b : b + col_count, :] for a in range(3) for b in range(3)
    ]
    return jnp.concatenate(pieces, axis=-1).reshape(-1, 9 * padded.shape[3])


def pad_columns(d_field):
    return jnp.pad(d_field, ((0, 0), (0, 0), (1, 1), (0, 0)))


def cell_forward(gate_input, cell_prev, channels):
    input_gate = jax.nn.sigmoid(gate_input[:, :channels])
    forget = jax.nn.sigmoid(gate_input[:, channels : 2 * channels])
    candidate = jnp.tanh(gate_input[:, 2 * channels : 3 * channels])
    output_gate = jax.nn.sigmoid(gate_input[:, 3 * channels :])
    cell_new = forget * cell_prev + input_gate * candidate
    hidden_new = (output_gate * jnp.tanh(cell_new)).astype(jnp.bfloat16)
    gate_values = jnp.concatenate([input_gate, forget, candidate, output_gate], axis=1)
    return (gate_values, cell_new, hidden_new)


def cell_backward(gate_values, cell_prev, cell_new, d_hidden, d_cell, channels):
    input_gate = gate_values[:, :channels]
    forget = gate_values[:, channels : 2 * channels]
    candidate = gate_values[:, 2 * channels : 3 * channels]
    output_gate = gate_values[:, 3 * channels :]
    squash = jnp.tanh(cell_new)
    d_total = d_cell + d_hidden * output_gate * (1.0 - squash * squash)
    d_gates = jnp.concatenate(
        [
            d_total * candidate * input_gate * (1.0 - input_gate),
            d_total * cell_prev * forget * (1.0 - forget),
            d_total * input_gate * (1.0 - candidate * candidate),
            d_hidden * squash * output_gate * (1.0 - output_gate),
        ],
        axis=1,
    ).astype(jnp.bfloat16)
    return (d_gates, d_total * forget)


def column_total(products, col_count, row_shift):
    result = products[:, :, 2 : 2 + col_count, row_shift, 0]
    for col_shift in range(1, 3):
        result = (
            result + products[:, :, 2 - col_shift : 2 - col_shift + col_count, row_shift, col_shift]
        )
    return result


def transpose_products(d_field, weight_matrix, channels):
    products = lax.dot_general(
        d_field, weight_matrix, (((3,), (1,)), ((), ())), preferred_element_type=jnp.float32
    )
    return products.reshape(d_field.shape[:3] + (3, 3, channels))


def per_device(
    syndromes, labels, stab_gate, bit_gate, forget_bias, conv_weight, query, readout_weight
):
    round_count, micro_count, shot_count, tile_rows, columns = syndromes.shape
    channels = conv_weight.shape[2]
    gate_units = conv_weight.shape[3]
    tile_sites = tile_rows * columns
    flat_rows = shot_count * tile_sites
    weight_matrix = conv_weight.reshape(9 * channels, gate_units)
    stab_rows = stab_gate.reshape(1, tile_sites, gate_units).astype(jnp.float32)
    forget_shift = jnp.concatenate(
        [jnp.zeros((channels,), jnp.float32), forget_bias, jnp.zeros((2 * channels,), jnp.float32)]
    )
    score_scale = 1.0 / math.sqrt(channels)
    field_shape = (shot_count, tile_rows, columns, channels)
    gate_shape = (shot_count, tile_rows, columns, gate_units)
    lead_tile = (lax.axis_index("tiles") == 0).astype(jnp.float32)

    def forward_round(recurrent, fired_bits):
        hidden_prev, cell_prev = recurrent
        hidden_rows = with_halo(hidden_prev, (("tiles", 1),), 1)
        hidden_pad = pad_columns(hidden_rows)
        gate_input = jnp.dot(
            make_patches(hidden_pad), weight_matrix, preferred_element_type=jnp.float32
        )
        gate_input = (
            gate_input.reshape(shot_count, tile_sites, gate_units)
            + stab_rows
            + fired_bits.astype(jnp.float32).reshape(shot_count, tile_sites, 1) * bit_gate
            + forget_shift
        )
        gate_values, cell_new, hidden_new = cell_forward(
            gate_input.reshape(flat_rows, gate_units), cell_prev, channels
        )
        return (
            (hidden_new.reshape(field_shape), cell_new),
            (hidden_pad, gate_values, cell_prev, cell_new, fired_bits),
        )

    def backward_round(state_carry, saved_items):
        d_hidden, d_cell, grad_weight, grad_stab_part, grad_fired, grad_keep = state_carry
        hidden_pad, gate_values, cell_prev, cell_new, fired_bits = saved_items
        d_gates, d_cell_prev = cell_backward(
            gate_values, cell_prev, cell_new, d_hidden, d_cell, channels
        )
        grad_weight = grad_weight + lax.dot_general(
            make_patches(hidden_pad),
            d_gates,
            (((0,), (0,)), ((), ())),
            preferred_element_type=jnp.float32,
        )
        grad_stab_part = grad_stab_part + jnp.sum(
            d_gates.reshape(shot_count, tile_sites, gate_units).astype(jnp.float32), axis=0
        )
        fired_row = fired_bits.astype(jnp.bfloat16).reshape(1, flat_rows)
        grad_fired = grad_fired + jnp.dot(fired_row, d_gates, preferred_element_type=jnp.float32)[0]
        grad_keep = grad_keep + jnp.sum(
            d_gates[:, channels : 2 * channels].astype(jnp.float32), axis=0
        )
        d_field = d_gates.reshape(gate_shape)
        d_rows = with_halo(d_field, (("tiles", 1),), 1)
        products = transpose_products(pad_columns(d_rows), weight_matrix, channels)
        d_hidden_prev = column_total(products[:, 2 : 2 + tile_rows], columns, 0)
        for row_shift in range(1, 3):
            d_hidden_prev = d_hidden_prev + column_total(
                products[:, 2 - row_shift : 2 - row_shift + tile_rows], columns, row_shift
            )
        return (
            (
                d_hidden_prev.reshape(flat_rows, channels),
                d_cell_prev,
                grad_weight,
                grad_stab_part,
                grad_fired,
                grad_keep,
            ),
            None,
        )

    def one_batch(totals, inputs):
        fired_rounds, batch_labels = inputs
        initial = (
            jnp.zeros(field_shape, jnp.bfloat16),
            jnp.zeros((flat_rows, channels), jnp.float32),
        )
        (hidden_last, unused_cell), saved = lax.scan(forward_round, initial, fired_rounds)
        hidden_full = hidden_last.astype(jnp.float32).reshape(shot_count, tile_sites, channels)
        scores = jnp.sum(hidden_full * query, axis=2) * score_scale
        exp_score = jnp.exp(scores)
        part_total = jnp.sum(exp_score, axis=1)
        part_numer = jnp.sum(exp_score[..., None] * hidden_full, axis=1)
        total_exp, numer = lax.psum((part_total, part_numer), "tiles")
        pooled = numer / total_exp[:, None]
        logit_value = jnp.sum(pooled * readout_weight, axis=1)
        targets = batch_labels.astype(jnp.float32)
        loss_part = jnp.sum(jax.nn.softplus(logit_value) - targets * logit_value)
        d_logit = jax.nn.sigmoid(logit_value) - targets
        d_pooled = d_logit[:, None] * readout_weight
        weight = exp_score / total_exp[:, None]
        d_score = weight * (
            jnp.sum(hidden_full * d_pooled[:, None, :], axis=2)
            - jnp.sum(pooled * d_pooled, axis=1)[:, None]
        )
        final_grad = (
            weight[..., None] * d_pooled[:, None, :] + d_score[..., None] * query * score_scale
        )
        query_part = score_scale * jnp.sum(d_score[..., None] * hidden_full, axis=(0, 1))
        readout_part = jnp.sum(d_logit[:, None] * pooled, axis=0)
        grad_weight, grad_stab_part, grad_fired, grad_keep, grad_query, grad_readout, loss_total = (
            totals
        )
        start_back = (
            final_grad.reshape(flat_rows, channels),
            jnp.zeros((flat_rows, channels), jnp.float32),
            grad_weight,
            grad_stab_part,
            grad_fired,
            grad_keep,
        )
        back_state, unused_out = lax.scan(backward_round, start_back, saved, reverse=True)
        return (
            (
                back_state[2],
                back_state[3],
                back_state[4],
                back_state[5],
                grad_query + query_part,
                grad_readout + readout_part,
                loss_total + loss_part,
            ),
            None,
        )

    zero_totals = (
        jnp.zeros((9 * channels, gate_units), jnp.float32),
        jnp.zeros((tile_sites, gate_units), jnp.float32),
        jnp.zeros((gate_units,), jnp.float32),
        jnp.zeros((channels,), jnp.float32),
        jnp.zeros((channels,), jnp.float32),
        jnp.zeros((channels,), jnp.float32),
        jnp.zeros((), jnp.float32),
    )
    batch_inputs = (jnp.swapaxes(syndromes, 0, 1), labels)
    sums, unused_out = lax.scan(one_batch, zero_totals, batch_inputs)
    grad_weight, grad_stab_part, grad_fired, grad_keep, grad_query, grad_readout, loss_total = sums
    stab_total = lax.psum(grad_stab_part.astype(jnp.bfloat16), "rounds").astype(jnp.float32)
    totals = lax.psum(
        (
            grad_weight,
            grad_fired,
            grad_keep,
            grad_query,
            grad_readout * lead_tile,
            loss_total * lead_tile,
        ),
        ("rounds", "tiles"),
    )
    return (
        totals[0].reshape(3, 3, channels, gate_units),
        stab_total.reshape(tile_rows, columns, gate_units),
        totals[1],
        totals[2],
        totals[3],
        totals[4],
        totals[5],
    )


def solution(mesh):
    in_specs = (
        P(None, None, "rounds", "tiles", None),
        P(None, "rounds"),
        P("tiles", None, None),
        P(),
        P(),
        P(),
        P(),
        P(),
    )
    out_specs = (P(), P("tiles", None, None), P(), P(), P(), P(), P())
    return jax.shard_map(
        per_device, mesh=mesh, in_specs=in_specs, out_specs=out_specs, check_vma=False
    )
```

profile of v0, /device:TPU:2, one launch (start us, length us, event | category | flops | bytes accessed | tf_op | source)
XLA Modules:
  0.0 1043.6 jit_solution(17618227137616668080)
XLA Ops:
  11.9 661.5 %while.108 = (s32[]{:T(128)}, f32[1152,512]{1,0:T(8,128)S(1)}, f32[128,512]{1,0:T(8,128)}, f32[512]{0:T(512)S(1)}, f32[128]{0:T(128)}, /*index=5*/f32[128]{0:T(1...) while((s32[]{:T(128)}, f32[1152,512]{1,0:T(8,128)S(1)}, ...), condition=%wide.region_15.16_spmd.clone, body=%wide.region_0.15_spmd.clone.sunk | while | flops 621755008 | bytes 24381452 | solution.py:227
  13.2 88.8 %while.109 = (s32[]{:T(128)}, bf16[1,2,64,128]{3,2,1,0:T(8,128)(2,1)S(1)}, f32[128,128]{1,0:T(8,128)S(1)}, bf16[8,1,4,66,128]{4,3,2,1,0:T(8,128)(2,1)}, f32[8,12...) while((s32[]{:T(128)}, ...), condition=%wide.region_2.2_spmd.clone, body=%wide.region_1.1_spmd.clone.sunk | while | flops 152739968 | bytes 4702967 | solution.py:169
  103.6 68.7 %all-reduce.5 = (f32[]{:T(128)}, f32[1,128]{1,0:T(1,128)S(1)}) all-reduce(f32[]{:T(128)} %get-tuple-element.1439, f32[1,128]{1,0:T(1,128)S(1)} %bitcast.186), channel_id=1, replica_groups=mesh['rounds'=8,'tiles'=32] {'tiles'}, use_global_device_ids=true, to_apply=%region_5.5 | all-reduce | flops 129 | bytes 1032 | tf_op jit(solution)/shard_map/while/body/eval_jaxpr/psum | solution.py:175
  185.9 148.6 %while.110 = (s32[]{:T(128)}, f32[128,128]{1,0:T(8,128)S(1)}, f32[128,128]{1,0:T(8,128)}, f32[1152,512]{1,0:T(8,128)S(1)}, f32[128,512]{1,0:T(8,128)}, /*index=5...) while((s32[]{:T(128)}, f32[128,128]{1,0:T(8,128)S(1)}, ...), condition=%wide.region_13.13_spmd.clone, body=%wide.region_11.12_spmd.clone.sunk | while | flops 468750976 | bytes 19420224 | solution.py:203
  189.8 6.0 collective-permute-start.2
  210.5 3.6 collective-permute-start.2
  228.7 3.6 collective-permute-start.2
  247.1 3.6 collective-permute-start.2
  265.3 3.6 collective-permute-start.2
  283.6 3.6 collective-permute-start.2
  301.9 3.6 collective-permute-start.2
  320.1 3.6 collective-permute-start.2
  335.8 100.8 %while.109 = (s32[]{:T(128)}, bf16[1,2,64,128]{3,2,1,0:T(8,128)(2,1)S(1)}, f32[128,128]{1,0:T(8,128)S(1)}, bf16[8,1,4,66,128]{4,3,2,1,0:T(8,128)(2,1)}, f32[8,12...) while((s32[]{:T(128)}, ...), condition=%wide.region_2.2_spmd.clone, body=%wide.region_1.1_spmd.clone.sunk | while | flops 152739968 | bytes 4702967 | solution.py:169
  335.9 3.6 collective-permute-start
  350.5 4.8 collective-permute-start.1
  362.1 5.8 collective-permute-start.1
  374.6 5.8 collective-permute-start.1
  387.2 5.8 collective-permute-start.1
  399.7 5.8 collective-permute-start.1
  412.3 6.3 collective-permute-start.1
  425.4 6.3 collective-permute-start.1
  438.3 72.4 %all-reduce.5 = (f32[]{:T(128)}, f32[1,128]{1,0:T(1,128)S(1)}) all-reduce(f32[]{:T(128)} %get-tuple-element.1439, f32[1,128]{1,0:T(1,128)S(1)} %bitcast.186), channel_id=1, replica_groups=mesh['rounds'=8,'tiles'=32] {'tiles'}, use_global_device_ids=true, to_apply=%region_5.5 | all-reduce | flops 129 | bytes 1032 | tf_op jit(solution)/shard_map/while/body/eval_jaxpr/psum | solution.py:175
  524.8 148.6 %while.110 = (s32[]{:T(128)}, f32[128,128]{1,0:T(8,128)S(1)}, f32[128,128]{1,0:T(8,128)}, f32[1152,512]{1,0:T(8,128)S(1)}, f32[128,512]{1,0:T(8,128)}, /*index=5...) while((s32[]{:T(128)}, f32[128,128]{1,0:T(8,128)S(1)}, ...), condition=%wide.region_13.13_spmd.clone, body=%wide.region_11.12_spmd.clone.sunk | while | flops 468750976 | bytes 19420224 | solution.py:203
  528.7 6.0 collective-permute-start.2
  549.4 3.6 collective-permute-start.2
  567.6 3.6 collective-permute-start.2
  585.9 3.6 collective-permute-start.2
  604.2 3.6 collective-permute-start.2
  622.5 3.6 collective-permute-start.2
  640.8 3.6 collective-permute-start.2
  676.7 94.3 %all-reduce.3 = (f32[512]{0:T(512)}, f32[128]{0:T(128)}, f32[128]{0:T(128)}, f32[128]{0:T(128)}, f32[]{:T(128)}) all-reduce(f32[512]{0:T(512)S(1)} %get-tuple-element.1688, f32[128]{0:T(128)S(1)} %copy-done.13, f32[128]{0:T(128)} %get-tuple-element.1690, ...), channel_id=1, replica_groups=mesh['rounds'=8,'tiles'=32] {'rounds','tiles'}, use_global_device_ids=true, to_apply=%region_18.19 | all-reduce | flops 897 | bytes 7176 | tf_op jit(solution)/shard_map/psum | solution.py:230
  772.7 260.7 %all-reduce.9.cloned.1.call-done = f32[3,3,128,512]{3,2,1,0:T(8,128)} async-done(((f32[3,3,128,512]{3,2,1,0:T(8,128)}), f32[3,3,128,512]{3,2,1,0:T(8,128)}) %all-reduce.9.cloned.1.call-update) | async-done | bytes 2359312 | tf_op jit(solution)/shard_map/psum | solution.py:230
  (1202 shorter events, 414.5 us)
Async XLA Ops:
  7.2 763.9 %all-reduce.11.cloned.1.call-start = ((), (), s32[]{:S(2)}) async-start(), calls=%async_computation.1 | async-start | bytes 262144 | tf_op jit(solution)/shard_map/psum | solution.py:229
  189.8 15.2 %collective-permute-start.2 = (bf16[1,1,64,512]{3,2,1,0:T(8,128)(2,1)}, bf16[1,1,64,512]{3,2,1,0:T(8,128)(2,1)}, u32[]{:S(2)}, u32[]{:S(2)}) collective-permute-start(bf16[1,1,64,512]{3,2,1,0:T(8,128)(2,1)} %get-tuple-element.1494), channel_id=1, source_target_pairs={{1,0},{2,1},{3,2},{4,3},{5,4},{6,5},{7,6},{8,7},{9,8},{10,9},{11,1... | collective-permute-start | bytes 196616 | tf_op jit(solution)/shard_map/while/body/eval_jaxpr/while/body/eval_jaxpr/ppermute | solution.py:18
  195.8 9.2 collective-permute-start.3
  210.5 12.8 %collective-permute-start.2 = (bf16[1,1,64,512]{3,2,1,0:T(8,128)(2,1)}, bf16[1,1,64,512]{3,2,1,0:T(8,128)(2,1)}, u32[]{:S(2)}, u32[]{:S(2)}) collective-permute-start(bf16[1,1,64,512]{3,2,1,0:T(8,128)(2,1)} %get-tuple-element.1494), channel_id=1, source_target_pairs={{1,0},{2,1},{3,2},{4,3},{5,4},{6,5},{7,6},{8,7},{9,8},{10,9},{11,1... | collective-permute-start | bytes 196616 | tf_op jit(solution)/shard_map/while/body/eval_jaxpr/while/body/eval_jaxpr/ppermute | solution.py:18
  214.1 9.2 collective-permute-start.3
  228.7 12.9 %collective-permute-start.2 = (bf16[1,1,64,512]{3,2,1,0:T(8,128)(2,1)}, bf16[1,1,64,512]{3,2,1,0:T(8,128)(2,1)}, u32[]{:S(2)}, u32[]{:S(2)}) collective-permute-start(bf16[1,1,64,512]{3,2,1,0:T(8,128)(2,1)} %get-tuple-element.1494), channel_id=1, source_target_pairs={{1,0},{2,1},{3,2},{4,3},{5,4},{6,5},{7,6},{8,7},{9,8},{10,9},{11,1... | collective-permute-start | bytes 196616 | tf_op jit(solution)/shard_map/while/body/eval_jaxpr/while/body/eval_jaxpr/ppermute | solution.py:18
  232.4 9.2 collective-permute-start.3
  247.1 12.8 %collective-permute-start.2 = (bf16[1,1,64,512]{3,2,1,0:T(8,128)(2,1)}, bf16[1,1,64,512]{3,2,1,0:T(8,128)(2,1)}, u32[]{:S(2)}, u32[]{:S(2)}) collective-permute-start(bf16[1,1,64,512]{3,2,1,0:T(8,128)(2,1)} %get-tuple-element.1494), channel_id=1, source_target_pairs={{1,0},{2,1},{3,2},{4,3},{5,4},{6,5},{7,6},{8,7},{9,8},{10,9},{11,1... | collective-permute-start | bytes 196616 | tf_op jit(solution)/shard_map/while/body/eval_jaxpr/while/body/eval_jaxpr/ppermute | solution.py:18
  250.7 9.2 collective-permute-start.3
  265.3 12.8 %collective-permute-start.2 = (bf16[1,1,64,512]{3,2,1,0:T(8,128)(2,1)}, bf16[1,1,64,512]{3,2,1,0:T(8,128)(2,1)}, u32[]{:S(2)}, u32[]{:S(2)}) collective-permute-start(bf16[1,1,64,512]{3,2,1,0:T(8,128)(2,1)} %get-tuple-element.1494), channel_id=1, source_target_pairs={{1,0},{2,1},{3,2},{4,3},{5,4},{6,5},{7,6},{8,7},{9,8},{10,9},{11,1... | collective-permute-start | bytes 196616 | tf_op jit(solution)/shard_map/while/body/eval_jaxpr/while/body/eval_jaxpr/ppermute | solution.py:18
  269.0 9.2 collective-permute-start.3
  283.6 12.8 %collective-permute-start.2 = (bf16[1,1,64,512]{3,2,1,0:T(8,128)(2,1)}, bf16[1,1,64,512]{3,2,1,0:T(8,128)(2,1)}, u32[]{:S(2)}, u32[]{:S(2)}) collective-permute-start(bf16[1,1,64,512]{3,2,1,0:T(8,128)(2,1)} %get-tuple-element.1494), channel_id=1, source_target_pairs={{1,0},{2,1},{3,2},{4,3},{5,4},{6,5},{7,6},{8,7},{9,8},{10,9},{11,1... | collective-permute-start | bytes 196616 | tf_op jit(solution)/shard_map/while/body/eval_jaxpr/while/body/eval_jaxpr/ppermute | solution.py:18
  287.2 9.2 collective-permute-start.3
  301.9 12.8 %collective-permute-start.2 = (bf16[1,1,64,512]{3,2,1,0:T(8,128)(2,1)}, bf16[1,1,64,512]{3,2,1,0:T(8,128)(2,1)}, u32[]{:S(2)}, u32[]{:S(2)}) collective-permute-start(bf16[1,1,64,512]{3,2,1,0:T(8,128)(2,1)} %get-tuple-element.1494), channel_id=1, source_target_pairs={{1,0},{2,1},{3,2},{4,3},{5,4},{6,5},{7,6},{8,7},{9,8},{10,9},{11,1... | collective-permute-start | bytes 196616 | tf_op jit(solution)/shard_map/while/body/eval_jaxpr/while/body/eval_jaxpr/ppermute | solution.py:18
  320.1 12.8 %collective-permute-start.2 = (bf16[1,1,64,512]{3,2,1,0:T(8,128)(2,1)}, bf16[1,1,64,512]{3,2,1,0:T(8,128)(2,1)}, u32[]{:S(2)}, u32[]{:S(2)}) collective-permute-start(bf16[1,1,64,512]{3,2,1,0:T(8,128)(2,1)} %get-tuple-element.1494), channel_id=1, source_target_pairs={{1,0},{2,1},{3,2},{4,3},{5,4},{6,5},{7,6},{8,7},{9,8},{10,9},{11,1... | collective-permute-start | bytes 196616 | tf_op jit(solution)/shard_map/while/body/eval_jaxpr/while/body/eval_jaxpr/ppermute | solution.py:18
  323.8 9.2 collective-permute-start.3
  528.7 15.2 %collective-permute-start.2 = (bf16[1,1,64,512]{3,2,1,0:T(8,128)(2,1)}, bf16[1,1,64,512]{3,2,1,0:T(8,128)(2,1)}, u32[]{:S(2)}, u32[]{:S(2)}) collective-permute-start(bf16[1,1,64,512]{3,2,1,0:T(8,128)(2,1)} %get-tuple-element.1494), channel_id=1, source_target_pairs={{1,0},{2,1},{3,2},{4,3},{5,4},{6,5},{7,6},{8,7},{9,8},{10,9},{11,1... | collective-permute-start | bytes 196616 | tf_op jit(solution)/shard_map/while/body/eval_jaxpr/while/body/eval_jaxpr/ppermute | solution.py:18
  534.7 9.2 collective-permute-start.3
  549.4 12.8 %collective-permute-start.2 = (bf16[1,1,64,512]{3,2,1,0:T(8,128)(2,1)}, bf16[1,1,64,512]{3,2,1,0:T(8,128)(2,1)}, u32[]{:S(2)}, u32[]{:S(2)}) collective-permute-start(bf16[1,1,64,512]{3,2,1,0:T(8,128)(2,1)} %get-tuple-element.1494), channel_id=1, source_target_pairs={{1,0},{2,1},{3,2},{4,3},{5,4},{6,5},{7,6},{8,7},{9,8},{10,9},{11,1... | collective-permute-start | bytes 196616 | tf_op jit(solution)/shard_map/while/body/eval_jaxpr/while/body/eval_jaxpr/ppermute | solution.py:18
  553.0 9.2 collective-permute-start.3
  567.6 12.8 %collective-permute-start.2 = (bf16[1,1,64,512]{3,2,1,0:T(8,128)(2,1)}, bf16[1,1,64,512]{3,2,1,0:T(8,128)(2,1)}, u32[]{:S(2)}, u32[]{:S(2)}) collective-permute-start(bf16[1,1,64,512]{3,2,1,0:T(8,128)(2,1)} %get-tuple-element.1494), channel_id=1, source_target_pairs={{1,0},{2,1},{3,2},{4,3},{5,4},{6,5},{7,6},{8,7},{9,8},{10,9},{11,1... | collective-permute-start | bytes 196616 | tf_op jit(solution)/shard_map/while/body/eval_jaxpr/while/body/eval_jaxpr/ppermute | solution.py:18
  571.3 9.2 collective-permute-start.3
  585.9 12.8 %collective-permute-start.2 = (bf16[1,1,64,512]{3,2,1,0:T(8,128)(2,1)}, bf16[1,1,64,512]{3,2,1,0:T(8,128)(2,1)}, u32[]{:S(2)}, u32[]{:S(2)}) collective-permute-start(bf16[1,1,64,512]{3,2,1,0:T(8,128)(2,1)} %get-tuple-element.1494), channel_id=1, source_target_pairs={{1,0},{2,1},{3,2},{4,3},{5,4},{6,5},{7,6},{8,7},{9,8},{10,9},{11,1... | collective-permute-start | bytes 196616 | tf_op jit(solution)/shard_map/while/body/eval_jaxpr/while/body/eval_jaxpr/ppermute | solution.py:18
  589.6 9.2 collective-permute-start.3
  604.2 12.8 %collective-permute-start.2 = (bf16[1,1,64,512]{3,2,1,0:T(8,128)(2,1)}, bf16[1,1,64,512]{3,2,1,0:T(8,128)(2,1)}, u32[]{:S(2)}, u32[]{:S(2)}) collective-permute-start(bf16[1,1,64,512]{3,2,1,0:T(8,128)(2,1)} %get-tuple-element.1494), channel_id=1, source_target_pairs={{1,0},{2,1},{3,2},{4,3},{5,4},{6,5},{7,6},{8,7},{9,8},{10,9},{11,1... | collective-permute-start | bytes 196616 | tf_op jit(solution)/shard_map/while/body/eval_jaxpr/while/body/eval_jaxpr/ppermute | solution.py:18
  607.9 9.2 collective-permute-start.3
  622.5 12.8 %collective-permute-start.2 = (bf16[1,1,64,512]{3,2,1,0:T(8,128)(2,1)}, bf16[1,1,64,512]{3,2,1,0:T(8,128)(2,1)}, u32[]{:S(2)}, u32[]{:S(2)}) collective-permute-start(bf16[1,1,64,512]{3,2,1,0:T(8,128)(2,1)} %get-tuple-element.1494), channel_id=1, source_target_pairs={{1,0},{2,1},{3,2},{4,3},{5,4},{6,5},{7,6},{8,7},{9,8},{10,9},{11,1... | collective-permute-start | bytes 196616 | tf_op jit(solution)/shard_map/while/body/eval_jaxpr/while/body/eval_jaxpr/ppermute | solution.py:18
  626.1 9.2 collective-permute-start.3
  640.8 12.8 %collective-permute-start.2 = (bf16[1,1,64,512]{3,2,1,0:T(8,128)(2,1)}, bf16[1,1,64,512]{3,2,1,0:T(8,128)(2,1)}, u32[]{:S(2)}, u32[]{:S(2)}) collective-permute-start(bf16[1,1,64,512]{3,2,1,0:T(8,128)(2,1)} %get-tuple-element.1494), channel_id=1, source_target_pairs={{1,0},{2,1},{3,2},{4,3},{5,4},{6,5},{7,6},{8,7},{9,8},{10,9},{11,1... | collective-permute-start | bytes 196616 | tf_op jit(solution)/shard_map/while/body/eval_jaxpr/while/body/eval_jaxpr/ppermute | solution.py:18
  659.0 12.8 %collective-permute-start.2 = (bf16[1,1,64,512]{3,2,1,0:T(8,128)(2,1)}, bf16[1,1,64,512]{3,2,1,0:T(8,128)(2,1)}, u32[]{:S(2)}, u32[]{:S(2)}) collective-permute-start(bf16[1,1,64,512]{3,2,1,0:T(8,128)(2,1)} %get-tuple-element.1494), channel_id=1, source_target_pairs={{1,0},{2,1},{3,2},{4,3},{5,4},{6,5},{7,6},{8,7},{9,8},{10,9},{11,1... | collective-permute-start | bytes 196616 | tf_op jit(solution)/shard_map/while/body/eval_jaxpr/while/body/eval_jaxpr/ppermute | solution.py:18
  662.7 9.2 collective-permute-start.3
  675.3 358.1 %all-reduce.9.cloned.1.call-start = ((), (), s32[]{:S(2)}) async-start(), calls=%async_computation | async-start | bytes 4718592 | tf_op jit(solution)/shard_map/psum | solution.py:230
  (214 other events, 1059.1 us)
Sparse Core Ops, SparseCore 0:
  675.4 90.3 all-reduce.10
  771.8 261.6 all-reduce.8
where the time goes:
time: 1050 us; the launch traced here: 1040 us
  waiting for transfers between devices  279 us (27%)
  blocking collectives  235 us (22%)
  starting transfers between devices  189 us (18%)
  other arithmetic  168 us (16%)
  matrix products  77.6 us (7%)
  local copies, waits for them, and re-layouts  65.3 us (6%)
  loops' own time  15.4 us (1%)
  between operations  14.1 us (1%)
    psum x1, waiting for transfers between devices, per_device(): lax.psum((grad_weight, grad_fired, grad_keep, grad_query, grad_readout *...  261 us
    psum x2, blocking collectives, one_batch(): total_exp, numer = lax.psum((part_total, part_numer), 'tiles')  141 us
    ppermute x32, starting transfers between devices, with_halo(): lax.ppermute(head, axis, [((i + 1) % count, i) for i in range(ends)])  95.1 us
    psum x1, blocking collectives, per_device(): lax.psum((grad_weight, grad_fired, grad_keep, grad_query, grad_readout *...  94.3 us
    ppermute x32, starting transfers between devices, with_halo(): lax.ppermute(tail, axis, [(i, (i + 1) % count) for i in range(ends)])  93.7 us
    dynamic_update_slice x48, other arithmetic, one_batch(): lax.scan(forward_round, initial, fired_rounds)  33.1 us
    squeeze x32, local copies, waits for them, and re-layouts, one_batch(): lax.scan(backward_round, start_back, saved, reverse=True)  29.9 us
    add x16, other arithmetic, backward_round(): grad_stab_part + jnp.sum(d_gates.reshape(shot_count, tile_sites, gate_uni...  28.7 us
  transfers between devices with their start and end apart: 66, of which 15 were waited for; matrix products, arithmetic and copies ran while one was open for 12% of the time, Pallas kernels for 0%

commit v1 on v0

--- a/solution.py
+++ b/solution.py
@@ -228,15 +228,18 @@
     grad_weight, grad_stab_part, grad_fired, grad_keep, grad_query, grad_readout, loss_total = sums
     stab_total = lax.psum(grad_stab_part.astype(jnp.bfloat16), "rounds").astype(jnp.float32)
     totals = lax.psum(
-        (
-            grad_weight,
-            grad_fired,
-            grad_keep,
-            grad_query,
-            grad_readout * lead_tile,
-            loss_total * lead_tile,
+        lax.psum(
+            (
+                grad_weight,
+                grad_fired,
+                grad_keep,
+                grad_query,
+                grad_readout * lead_tile,
+                loss_total * lead_tile,
+            ),
+            "rounds",
         ),
-        ("rounds", "tiles"),
+        "tiles",
     )
     return (
         totals[0].reshape(3, 3, channels, gate_units),

time: 1050 us -> 988 us (0.941)
  waiting for transfers between devices: 279 us -> 232 us
  blocking collectives: 235 us -> 216 us
    psum x1, waiting for transfers between devices: 261 us -> 99.9 us  [per_device(): lax.psum((grad_weight, grad_fired, grad_keep, grad_query, grad_readout *...]
    psum x0 -> x1, waiting for transfers between devices: none -> 115 us  [per_device(): lax.psum(lax.psum((grad_weight, grad_fired, grad_keep, grad_query, grad_r...]
    psum x1, blocking collectives: 94.3 us -> 16.8 us  [per_device(): lax.psum((grad_weight, grad_fired, grad_keep, grad_query, grad_readout *...]
    psum x0 -> x1, blocking collectives: none -> 58.3 us  [per_device(): lax.psum(lax.psum((grad_weight, grad_fired, grad_keep, grad_query, grad_r...]
  transfers between devices with their start and end apart: 66 -> 67, of which waited for: 15 -> 17; matrix products, arithmetic and copies ran while one was open for 12% -> 13% of each run, Pallas kernels for 0% -> 0%
where the time goes in v1:
time: 988 us; the launch traced here: 980 us
  waiting for transfers between devices  232 us (23%)
  blocking collectives  216 us (22%)
  starting transfers between devices  189 us (19%)
  other arithmetic  167 us (17%)
  matrix products  77.6 us (8%)
  local copies, waits for them, and re-layouts  66.7 us (7%)
  loops' own time  17.1 us (2%)
  between operations  13.8 us (1%)
    psum x2, blocking collectives, one_batch(): total_exp, numer = lax.psum((part_total, part_numer), 'tiles')  141 us
    psum x1, waiting for transfers between devices, per_device(): lax.psum(lax.psum((grad_weight, grad_fired, grad_keep, grad_query, grad_r...  115 us
    psum x1, waiting for transfers between devices, per_device(): lax.psum((grad_weight, grad_fired, grad_keep, grad_query, grad_readout *...  99.9 us
    ppermute x32, starting transfers between devices, with_halo(): lax.ppermute(head, axis, [((i + 1) % count, i) for i in range(ends)])  95.2 us
    ppermute x32, starting transfers between devices, with_halo(): lax.ppermute(tail, axis, [(i, (i + 1) % count) for i in range(ends)])  93.7 us
    psum x1, blocking collectives, per_device(): lax.psum(lax.psum((grad_weight, grad_fired, grad_keep, grad_query, grad_r...  58.3 us
    dynamic_update_slice x48, other arithmetic, one_batch(): lax.scan(forward_round, initial, fired_rounds)  33.1 us
    squeeze x32, local copies, waits for them, and re-layouts, one_batch(): lax.scan(backward_round, start_back, saved, reverse=True)  29.9 us
  transfers between devices with their start and end apart: 67, of which 17 were waited for; matrix products, arithmetic and copies ran while one was open for 13% of the time, Pallas kernels for 0%

profile of v1, /device:TPU:2, one launch (start us, length us, event | category | flops | bytes accessed | tf_op | source)
XLA Modules:
  0.0 979.6 jit_solution(18416763440789632061)
XLA Ops:
  11.9 662.5 %while.108 = (s32[]{:T(128)}, f32[1152,512]{1,0:T(8,128)S(1)}, f32[128,512]{1,0:T(8,128)}, f32[512]{0:T(512)S(1)}, f32[128]{0:T(128)}, /*index=5*/f32[128]{0:T(1...) while((s32[]{:T(128)}, f32[1152,512]{1,0:T(8,128)S(1)}, ...), condition=%wide.region_15.16_spmd.clone, body=%wide.region_0.15_spmd.clone.sunk | while | flops 621755008 | bytes 24381452 | solution.py:227
  13.2 88.8 %while.109 = (s32[]{:T(128)}, bf16[1,2,64,128]{3,2,1,0:T(8,128)(2,1)S(1)}, f32[128,128]{1,0:T(8,128)S(1)}, bf16[8,1,4,66,128]{4,3,2,1,0:T(8,128)(2,1)}, f32[8,12...) while((s32[]{:T(128)}, ...), condition=%wide.region_2.2_spmd.clone, body=%wide.region_1.1_spmd.clone.sunk | while | flops 152739968 | bytes 4702967 | solution.py:169
  103.6 68.7 %all-reduce.6 = (f32[]{:T(128)}, f32[1,128]{1,0:T(1,128)S(1)}) all-reduce(f32[]{:T(128)} %get-tuple-element.1444, f32[1,128]{1,0:T(1,128)S(1)} %bitcast.186), channel_id=1, replica_groups=mesh['rounds'=8,'tiles'=32] {'tiles'}, use_global_device_ids=true, to_apply=%region_5.5 | all-reduce | flops 129 | bytes 1032 | tf_op jit(solution)/shard_map/while/body/eval_jaxpr/psum | solution.py:175
  186.5 148.4 %while.110 = (s32[]{:T(128)}, f32[128,128]{1,0:T(8,128)S(1)}, f32[128,128]{1,0:T(8,128)}, f32[1152,512]{1,0:T(8,128)S(1)}, f32[128,512]{1,0:T(8,128)}, /*index=5...) while((s32[]{:T(128)}, f32[128,128]{1,0:T(8,128)S(1)}, ...), condition=%wide.region_13.13_spmd.clone, body=%wide.region_11.12_spmd.clone.sunk | while | flops 468750976 | bytes 19420224 | solution.py:203
  190.4 6.0 collective-permute-start.2
  229.3 3.6 collective-permute-start.2
  247.6 3.6 collective-permute-start.2
  265.8 3.6 collective-permute-start.2
  284.0 3.6 collective-permute-start.2
  320.6 3.6 collective-permute-start.2
  336.3 100.8 %while.109 = (s32[]{:T(128)}, bf16[1,2,64,128]{3,2,1,0:T(8,128)(2,1)S(1)}, f32[128,128]{1,0:T(8,128)S(1)}, bf16[8,1,4,66,128]{4,3,2,1,0:T(8,128)(2,1)}, f32[8,12...) while((s32[]{:T(128)}, ...), condition=%wide.region_2.2_spmd.clone, body=%wide.region_1.1_spmd.clone.sunk | while | flops 152739968 | bytes 4702967 | solution.py:169
  336.3 3.6 collective-permute-start
  351.0 4.8 collective-permute-start.1
  362.5 5.7 collective-permute-start.1
  375.1 5.8 collective-permute-start.1
  387.7 5.7 collective-permute-start.1
  400.2 5.8 collective-permute-start.1
  412.8 6.4 collective-permute-start.1
  425.9 6.3 collective-permute-start.1
  438.7 72.4 %all-reduce.6 = (f32[]{:T(128)}, f32[1,128]{1,0:T(1,128)S(1)}) all-reduce(f32[]{:T(128)} %get-tuple-element.1444, f32[1,128]{1,0:T(1,128)S(1)} %bitcast.186), channel_id=1, replica_groups=mesh['rounds'=8,'tiles'=32] {'tiles'}, use_global_device_ids=true, to_apply=%region_5.5 | all-reduce | flops 129 | bytes 1032 | tf_op jit(solution)/shard_map/while/body/eval_jaxpr/psum | solution.py:175
  525.9 148.4 %while.110 = (s32[]{:T(128)}, f32[128,128]{1,0:T(8,128)S(1)}, f32[128,128]{1,0:T(8,128)}, f32[1152,512]{1,0:T(8,128)S(1)}, f32[128,512]{1,0:T(8,128)}, /*index=5...) while((s32[]{:T(128)}, f32[128,128]{1,0:T(8,128)S(1)}, ...), condition=%wide.region_13.13_spmd.clone, body=%wide.region_11.12_spmd.clone.sunk | while | flops 468750976 | bytes 19420224 | solution.py:203
  529.8 6.0 collective-permute-start.2
  550.4 3.6 collective-permute-start.2
  568.6 3.6 collective-permute-start.2
  586.9 3.6 collective-permute-start.2
  605.2 3.6 collective-permute-start.2
  623.4 3.6 collective-permute-start.2
  660.0 3.6 collective-permute-start.2
  677.5 99.9 %all-reduce.11.cloned.1.call-done = f32[1152,512]{1,0:T(8,128)} async-done(((f32[1152,512]{1,0:T(8,128)}), f32[1152,512]{1,0:T(8,128)}) %all-reduce.11.cloned.1.call-update) | async-done | bytes 2359312 | tf_op jit(solution)/shard_map/psum | solution.py:231
  778.1 16.8 %all-reduce.4 = (f32[512]{0:T(512)S(1)}, f32[128]{0:T(128)S(1)}, f32[128]{0:T(128)S(1)}, f32[128]{0:T(128)S(1)}, f32[]{:T(128)}) all-reduce(f32[512]{0:T(512)S(1)} %get-tuple-element.1697, f32[128]{0:T(128)S(1)} %copy-done.13, f32[128]{0:T(128)} %get-tuple-element.1699, ...), channel_id=1, replica_groups=mesh['rounds'=8,'tiles'=32] {'rounds'}, use_global_device_ids=true, to_apply=%region_19.20 | all-reduce | flops 897 | bytes 7176 | tf_op jit(solution)/shard_map/psum | solution.py:231
  794.9 58.3 %all-reduce.3 = (f32[512]{0:T(512)}, f32[128]{0:T(128)}, f32[128]{0:T(128)}, f32[128]{0:T(128)}, f32[]{:T(128)}) all-reduce(f32[512]{0:T(512)S(1)} %get-tuple-element.1095, f32[128]{0:T(128)S(1)} %get-tuple-element.1096, f32[128]{0:T(128)S(1)} %get-tuple-element.1097, ...), channel_id=1, replica_groups=mesh['rounds'=8,'tiles'=32] {'tiles'}, use_global_device_ids=true, to_apply=%region_20.21 | all-reduce | flops 897 | bytes 7176 | tf_op jit(solution)/shard_map/psum | solution.py:230
  854.9 114.9 %all-reduce.13.cloned.1.call-done = f32[3,3,128,512]{3,2,1,0:T(8,128)} async-done(((f32[3,3,128,512]{3,2,1,0:T(8,128)}), f32[3,3,128,512]{3,2,1,0:T(8,128)}) %all-reduce.13.cloned.1.call-update) | async-done | bytes 2359312 | tf_op jit(solution)/shard_map/psum | solution.py:230
  (1206 shorter events, 421.6 us)
Async XLA Ops:
  7.2 770.2 %all-reduce.11.cloned.1.call-start = ((), (), s32[]{:S(2)}) async-start(), calls=%async_computation | async-start | bytes 4718592 | tf_op jit(solution)/shard_map/psum | solution.py:231
  190.4 15.2 %collective-permute-start.2 = (bf16[1,1,64,512]{3,2,1,0:T(8,128)(2,1)}, bf16[1,1,64,512]{3,2,1,0:T(8,128)(2,1)}, u32[]{:S(2)}, u32[]{:S(2)}) collective-permute-start(bf16[1,1,64,512]{3,2,1,0:T(8,128)(2,1)} %get-tuple-element.1499), channel_id=1, source_target_pairs={{1,0},{2,1},{3,2},{4,3},{5,4},{6,5},{7,6},{8,7},{9,8},{10,9},{11,1... | collective-permute-start | bytes 196616 | tf_op jit(solution)/shard_map/while/body/eval_jaxpr/while/body/eval_jaxpr/ppermute | solution.py:18
  196.4 9.2 collective-permute-start.3
  211.0 12.8 %collective-permute-start.2 = (bf16[1,1,64,512]{3,2,1,0:T(8,128)(2,1)}, bf16[1,1,64,512]{3,2,1,0:T(8,128)(2,1)}, u32[]{:S(2)}, u32[]{:S(2)}) collective-permute-start(bf16[1,1,64,512]{3,2,1,0:T(8,128)(2,1)} %get-tuple-element.1499), channel_id=1, source_target_pairs={{1,0},{2,1},{3,2},{4,3},{5,4},{6,5},{7,6},{8,7},{9,8},{10,9},{11,1... | collective-permute-start | bytes 196616 | tf_op jit(solution)/shard_map/while/body/eval_jaxpr/while/body/eval_jaxpr/ppermute | solution.py:18
  229.3 12.9 %collective-permute-start.2 = (bf16[1,1,64,512]{3,2,1,0:T(8,128)(2,1)}, bf16[1,1,64,512]{3,2,1,0:T(8,128)(2,1)}, u32[]{:S(2)}, u32[]{:S(2)}) collective-permute-start(bf16[1,1,64,512]{3,2,1,0:T(8,128)(2,1)} %get-tuple-element.1499), channel_id=1, source_target_pairs={{1,0},{2,1},{3,2},{4,3},{5,4},{6,5},{7,6},{8,7},{9,8},{10,9},{11,1... | collective-permute-start | bytes 196616 | tf_op jit(solution)/shard_map/while/body/eval_jaxpr/while/body/eval_jaxpr/ppermute | solution.py:18
  232.9 9.2 collective-permute-start.3
  247.6 12.8 %collective-permute-start.2 = (bf16[1,1,64,512]{3,2,1,0:T(8,128)(2,1)}, bf16[1,1,64,512]{3,2,1,0:T(8,128)(2,1)}, u32[]{:S(2)}, u32[]{:S(2)}) collective-permute-start(bf16[1,1,64,512]{3,2,1,0:T(8,128)(2,1)} %get-tuple-element.1499), channel_id=1, source_target_pairs={{1,0},{2,1},{3,2},{4,3},{5,4},{6,5},{7,6},{8,7},{9,8},{10,9},{11,1... | collective-permute-start | bytes 196616 | tf_op jit(solution)/shard_map/while/body/eval_jaxpr/while/body/eval_jaxpr/ppermute | solution.py:18
  251.2 9.2 collective-permute-start.3
  265.8 12.8 %collective-permute-start.2 = (bf16[1,1,64,512]{3,2,1,0:T(8,128)(2,1)}, bf16[1,1,64,512]{3,2,1,0:T(8,128)(2,1)}, u32[]{:S(2)}, u32[]{:S(2)}) collective-permute-start(bf16[1,1,64,512]{3,2,1,0:T(8,128)(2,1)} %get-tuple-element.1499), channel_id=1, source_target_pairs={{1,0},{2,1},{3,2},{4,3},{5,4},{6,5},{7,6},{8,7},{9,8},{10,9},{11,1... | collective-permute-start | bytes 196616 | tf_op jit(solution)/shard_map/while/body/eval_jaxpr/while/body/eval_jaxpr/ppermute | solution.py:18
  269.5 9.2 collective-permute-start.3
  284.0 12.8 %collective-permute-start.2 = (bf16[1,1,64,512]{3,2,1,0:T(8,128)(2,1)}, bf16[1,1,64,512]{3,2,1,0:T(8,128)(2,1)}, u32[]{:S(2)}, u32[]{:S(2)}) collective-permute-start(bf16[1,1,64,512]{3,2,1,0:T(8,128)(2,1)} %get-tuple-element.1499), channel_id=1, source_target_pairs={{1,0},{2,1},{3,2},{4,3},{5,4},{6,5},{7,6},{8,7},{9,8},{10,9},{11,1... | collective-permute-start | bytes 196616 | tf_op jit(solution)/shard_map/while/body/eval_jaxpr/while/body/eval_jaxpr/ppermute | solution.py:18
  287.7 9.2 collective-permute-start.3
  302.3 12.8 %collective-permute-start.2 = (bf16[1,1,64,512]{3,2,1,0:T(8,128)(2,1)}, bf16[1,1,64,512]{3,2,1,0:T(8,128)(2,1)}, u32[]{:S(2)}, u32[]{:S(2)}) collective-permute-start(bf16[1,1,64,512]{3,2,1,0:T(8,128)(2,1)} %get-tuple-element.1499), channel_id=1, source_target_pairs={{1,0},{2,1},{3,2},{4,3},{5,4},{6,5},{7,6},{8,7},{9,8},{10,9},{11,1... | collective-permute-start | bytes 196616 | tf_op jit(solution)/shard_map/while/body/eval_jaxpr/while/body/eval_jaxpr/ppermute | solution.py:18
  305.9 9.2 collective-permute-start.3
  320.6 12.9 %collective-permute-start.2 = (bf16[1,1,64,512]{3,2,1,0:T(8,128)(2,1)}, bf16[1,1,64,512]{3,2,1,0:T(8,128)(2,1)}, u32[]{:S(2)}, u32[]{:S(2)}) collective-permute-start(bf16[1,1,64,512]{3,2,1,0:T(8,128)(2,1)} %get-tuple-element.1499), channel_id=1, source_target_pairs={{1,0},{2,1},{3,2},{4,3},{5,4},{6,5},{7,6},{8,7},{9,8},{10,9},{11,1... | collective-permute-start | bytes 196616 | tf_op jit(solution)/shard_map/while/body/eval_jaxpr/while/body/eval_jaxpr/ppermute | solution.py:18
  324.2 9.2 collective-permute-start.3
  529.8 15.2 %collective-permute-start.2 = (bf16[1,1,64,512]{3,2,1,0:T(8,128)(2,1)}, bf16[1,1,64,512]{3,2,1,0:T(8,128)(2,1)}, u32[]{:S(2)}, u32[]{:S(2)}) collective-permute-start(bf16[1,1,64,512]{3,2,1,0:T(8,128)(2,1)} %get-tuple-element.1499), channel_id=1, source_target_pairs={{1,0},{2,1},{3,2},{4,3},{5,4},{6,5},{7,6},{8,7},{9,8},{10,9},{11,1... | collective-permute-start | bytes 196616 | tf_op jit(solution)/shard_map/while/body/eval_jaxpr/while/body/eval_jaxpr/ppermute | solution.py:18
  535.8 9.2 collective-permute-start.3
  550.4 12.8 %collective-permute-start.2 = (bf16[1,1,64,512]{3,2,1,0:T(8,128)(2,1)}, bf16[1,1,64,512]{3,2,1,0:T(8,128)(2,1)}, u32[]{:S(2)}, u32[]{:S(2)}) collective-permute-start(bf16[1,1,64,512]{3,2,1,0:T(8,128)(2,1)} %get-tuple-element.1499), channel_id=1, source_target_pairs={{1,0},{2,1},{3,2},{4,3},{5,4},{6,5},{7,6},{8,7},{9,8},{10,9},{11,1... | collective-permute-start | bytes 196616 | tf_op jit(solution)/shard_map/while/body/eval_jaxpr/while/body/eval_jaxpr/ppermute | solution.py:18
  568.6 12.9 %collective-permute-start.2 = (bf16[1,1,64,512]{3,2,1,0:T(8,128)(2,1)}, bf16[1,1,64,512]{3,2,1,0:T(8,128)(2,1)}, u32[]{:S(2)}, u32[]{:S(2)}) collective-permute-start(bf16[1,1,64,512]{3,2,1,0:T(8,128)(2,1)} %get-tuple-element.1499), channel_id=1, source_target_pairs={{1,0},{2,1},{3,2},{4,3},{5,4},{6,5},{7,6},{8,7},{9,8},{10,9},{11,1... | collective-permute-start | bytes 196616 | tf_op jit(solution)/shard_map/while/body/eval_jaxpr/while/body/eval_jaxpr/ppermute | solution.py:18
  572.3 9.2 collective-permute-start.3
  586.9 12.8 %collective-permute-start.2 = (bf16[1,1,64,512]{3,2,1,0:T(8,128)(2,1)}, bf16[1,1,64,512]{3,2,1,0:T(8,128)(2,1)}, u32[]{:S(2)}, u32[]{:S(2)}) collective-permute-start(bf16[1,1,64,512]{3,2,1,0:T(8,128)(2,1)} %get-tuple-element.1499), channel_id=1, source_target_pairs={{1,0},{2,1},{3,2},{4,3},{5,4},{6,5},{7,6},{8,7},{9,8},{10,9},{11,1... | collective-permute-start | bytes 196616 | tf_op jit(solution)/shard_map/while/body/eval_jaxpr/while/body/eval_jaxpr/ppermute | solution.py:18
  590.6 9.2 collective-permute-start.3
  605.2 12.8 %collective-permute-start.2 = (bf16[1,1,64,512]{3,2,1,0:T(8,128)(2,1)}, bf16[1,1,64,512]{3,2,1,0:T(8,128)(2,1)}, u32[]{:S(2)}, u32[]{:S(2)}) collective-permute-start(bf16[1,1,64,512]{3,2,1,0:T(8,128)(2,1)} %get-tuple-element.1499), channel_id=1, source_target_pairs={{1,0},{2,1},{3,2},{4,3},{5,4},{6,5},{7,6},{8,7},{9,8},{10,9},{11,1... | collective-permute-start | bytes 196616 | tf_op jit(solution)/shard_map/while/body/eval_jaxpr/while/body/eval_jaxpr/ppermute | solution.py:18
  623.4 12.8 %collective-permute-start.2 = (bf16[1,1,64,512]{3,2,1,0:T(8,128)(2,1)}, bf16[1,1,64,512]{3,2,1,0:T(8,128)(2,1)}, u32[]{:S(2)}, u32[]{:S(2)}) collective-permute-start(bf16[1,1,64,512]{3,2,1,0:T(8,128)(2,1)} %get-tuple-element.1499), channel_id=1, source_target_pairs={{1,0},{2,1},{3,2},{4,3},{5,4},{6,5},{7,6},{8,7},{9,8},{10,9},{11,1... | collective-permute-start | bytes 196616 | tf_op jit(solution)/shard_map/while/body/eval_jaxpr/while/body/eval_jaxpr/ppermute | solution.py:18
  627.1 9.2 collective-permute-start.3
  641.7 12.8 %collective-permute-start.2 = (bf16[1,1,64,512]{3,2,1,0:T(8,128)(2,1)}, bf16[1,1,64,512]{3,2,1,0:T(8,128)(2,1)}, u32[]{:S(2)}, u32[]{:S(2)}) collective-permute-start(bf16[1,1,64,512]{3,2,1,0:T(8,128)(2,1)} %get-tuple-element.1499), channel_id=1, source_target_pairs={{1,0},{2,1},{3,2},{4,3},{5,4},{6,5},{7,6},{8,7},{9,8},{10,9},{11,1... | collective-permute-start | bytes 196616 | tf_op jit(solution)/shard_map/while/body/eval_jaxpr/while/body/eval_jaxpr/ppermute | solution.py:18
  645.3 9.2 collective-permute-start.3
  660.0 12.9 %collective-permute-start.2 = (bf16[1,1,64,512]{3,2,1,0:T(8,128)(2,1)}, bf16[1,1,64,512]{3,2,1,0:T(8,128)(2,1)}, u32[]{:S(2)}, u32[]{:S(2)}) collective-permute-start(bf16[1,1,64,512]{3,2,1,0:T(8,128)(2,1)} %get-tuple-element.1499), channel_id=1, source_target_pairs={{1,0},{2,1},{3,2},{4,3},{5,4},{6,5},{7,6},{8,7},{9,8},{10,9},{11,1... | collective-permute-start | bytes 196616 | tf_op jit(solution)/shard_map/while/body/eval_jaxpr/while/body/eval_jaxpr/ppermute | solution.py:18
  663.6 9.2 collective-permute-start.3
  675.8 177.5 %all-reduce.15.cloned.1.call-start = ((), (), s32[]{:S(2)}) async-start(), calls=%async_computation.2 | async-start | bytes 262144 | tf_op jit(solution)/shard_map/psum | solution.py:229
  677.5 292.3 %all-reduce.13.cloned.1.call-start = ((), (), s32[]{:S(2)}) async-start(), calls=%async_computation.1 | async-start | bytes 4718592 | tf_op jit(solution)/shard_map/psum | solution.py:230
  (215 other events, 1167.9 us)
Sparse Core Ops, SparseCore 0:
  675.9 101.4 all-reduce.10
  779.7 71.1 all-reduce.14
  854.3 115.4 all-reduce.12
